TPU v7x, 512 devices: a whole 4x8x8 slice. The times are simulated.
512 devices in a mesh: seq: 64 (over z, y_hi, core), head: 8 (over x, y_lo).
Axes of the slice: x: 4, y: 8 (y_hi: 4, y_lo: 2; y = y_hi * 2 + y_lo), z: 8, core: 2. Of those that a mesh axis runs over, the one named last changes fastest.
Arguments:
- block_query_rows: bfloat16 [8192, 5120], P('seq', 'head'), may hold values from -180 to 180
- block_key_rows: bfloat16 [8192, 1024], P('seq', 'head'), may hold values from -6 to 6
- block_value_rows: bfloat16 [8192, 1024], P('seq', 'head'), may hold values from -6 to 6
- stretch_segments: int32 [8192], P('seq'), may hold values from 0 to 15, never falling along the last dimension, each value on 1 to 6144 neighbouring positions
- residual: bfloat16 [8192, 5120], P('seq', 'head'), may hold values from -6 to 6
- out_weight: bfloat16 [5120, 5120], P('head', 'seq'), may hold values from -0.25 to 0.25
- cache_by_prefill: bfloat16 [2, 2, 2048, 16, 1024], P(None, None, 'seq', None, 'head'), may hold values from -6 to 6
- request_pages: int32 [128], replicated, may hold values from 1 to 64, as said below
- request_owner: int32 [128], replicated, may hold values from 0 to 63, as said below
Outputs:
- layer_out: bfloat16 [8192, 5120], P('seq', 'head')
- cache_decode: bfloat16 [2, 2, 4096, 16, 1024], P(None, None, 'seq', None, 'head')
Inputs may be any that keep to these rules, and one draw needn't show every extreme that they name: `stretch_segments`: each request of the block holds at most 6144 tokens, and some request exactly that many. `request_pages`: the requests of one decode device hold at most 64 pages together, and those of some device exactly 64. `request_owner`: never falls along the requests; every device owns at least one request.
All inputs are finite; a program needn't handle non-finite values.
Results may differ from a plain program's by a relative error of at most 0.0065.
Values may be sent and summed in bfloat16 or wider, within the bound.
A program may use at most 128 MiB of HBM per device.

v0:
```python
import jax
import jax.numpy as jnp
from jax import lax
from jax.sharding import PartitionSpec as P

HEAD_SIZE = 128


def on_device(
    block_query_rows,
    block_key_rows,
    block_value_rows,
    stretch_segments,
    residual,
    out_weight,
    cache_by_prefill,
    request_pages,
    request_owner,
):
    seq_count = lax.axis_size("seq")
    seq_place = lax.axis_index("seq")
    rows = block_query_rows.shape[0]
    kv_local = block_key_rows.shape[1] // HEAD_SIZE
    query_groups = block_query_rows.shape[1] // block_key_rows.shape[1]
    query_four = block_query_rows.reshape(rows, kv_local, query_groups, HEAD_SIZE)
    query_place = seq_place * rows + jnp.arange(rows, dtype=jnp.int32)
    scale = HEAD_SIZE ** (-0.5)
    key_part = lax.all_gather(block_key_rows, "seq", axis=0, tiled=True)
    value_part = lax.all_gather(block_value_rows, "seq", axis=0, tiled=True)
    segment_part = lax.all_gather(stretch_segments, "seq", axis=0, tiled=True)
    count = key_part.shape[0]
    key_place = jnp.arange(count, dtype=jnp.int32)
    allowed = (
        (stretch_segments[:, None] == segment_part[None, :])
        & (query_place[:, None] >= key_place[None, :])
        & (key_place[None, :] >= 0)
    )
    running_max = jnp.full((kv_local, query_groups, rows), -1e30, jnp.float32)
    key_three = key_part.reshape(count, kv_local, HEAD_SIZE)
    value_three = value_part.reshape(count, kv_local, HEAD_SIZE)
    scores = (
        jnp.einsum("tkgd,pkd->kgtp", query_four, key_three, preferred_element_type=jnp.float32)
        * scale
    )
    masked = jnp.where(allowed, scores, -1e30)
    new_max = jnp.maximum(running_max, jnp.max(masked, axis=-1))
    weights = jnp.where(allowed, jnp.exp(masked - new_max[..., None]), 0.0)
    new_sum = jnp.sum(weights, axis=-1)
    contribution = jnp.einsum(
        "kgtp,pkd->kgtd",
        weights.astype(jnp.bfloat16),
        value_three,
        preferred_element_type=jnp.float32,
    )
    attention = (
        jnp.transpose(contribution / new_sum[..., None], (2, 0, 1, 3))
        .reshape(rows, -1)
        .astype(jnp.bfloat16)
    )
    partial_value = jnp.dot(
        attention,
        lax.all_gather(out_weight, "seq", axis=1, tiled=True),
        preferred_element_type=jnp.float32,
    )
    feature_width = partial_value.shape[1] // lax.axis_size("head")
    total = lax.psum(partial_value.astype(jnp.bfloat16), "head").astype(jnp.float32)
    mine = lax.dynamic_slice_in_dim(total, lax.axis_index("head") * feature_width, feature_width, 1)
    layer_out = (residual.astype(jnp.float32) + mine).astype(jnp.bfloat16)
    local_pages = cache_by_prefill.shape[2]
    capacity = 2 * local_pages
    per_pair = capacity // seq_count
    owners = jnp.arange(seq_count, dtype=jnp.int32)
    run_pages = jnp.sum(
        jnp.where(request_owner[None, :] == owners[:, None], request_pages[None, :], 0), axis=1
    )
    run_start = jnp.sum(
        jnp.where(request_owner[None, :] < owners[:, None], request_pages[None, :], 0), axis=1
    )
    pair_slots = jnp.arange(per_pair, dtype=jnp.int32)
    offset = (seq_place - run_start) % seq_count
    slot_index = pair_slots[None, :] * seq_count + offset[:, None]
    sending = slot_index < run_pages[:, None]
    local_index = pair_slots[None, :] + ((run_start + offset - seq_place) // seq_count)[:, None]
    local_index = jnp.where(sending, local_index, 0).reshape(-1)
    picked = jnp.take(cache_by_prefill, local_index, axis=2)
    outgoing = jnp.where(
        sending.reshape(-1)[None, None, :, None, None], picked, jnp.zeros_like(picked)
    )
    incoming = lax.all_to_all(outgoing, "seq", split_axis=2, concat_axis=2, tiled=True)
    layers, pair_kv, _, page_len, width = incoming.shape
    arranged = jnp.swapaxes(
        incoming.reshape(layers, pair_kv, seq_count, per_pair, page_len, width), 2, 3
    )
    my_start = run_start[seq_place]
    my_pages = run_pages[seq_place]
    rotated = jnp.roll(arranged, -my_start, axis=3).reshape(
        layers, pair_kv, capacity, page_len, width
    )
    keep = jnp.arange(capacity, dtype=jnp.int32) < my_pages
    cache_decode = jnp.where(keep[None, None, :, None, None], rotated, jnp.zeros_like(rotated))
    return (layer_out, cache_decode)


def solution(mesh):
    return jax.shard_map(
        on_device,
        mesh=mesh,
        in_specs=(
            P("seq", "head"),
            P("seq", "head"),
            P("seq", "head"),
            P("seq"),
            P("seq", "head"),
            P("head", "seq"),
            P(None, None, "seq", None, "head"),
            P(),
            P(),
        ),
        out_specs=(P("seq", "head"), P(None, None, "seq", None, "head")),
        check_vma=False,
    )
```

profile of v0, /device:TPU:16, one launch (start us, length us, event | category | flops | bytes accessed | tf_op | source)
XLA Modules:
  0.0 391.2 jit_solution(16656007094815539979)
XLA Ops:
  7.2 0.0 copy-start
  7.2 0.0 all-gather.5.cloned.1.call-start
  7.2 0.7 all-gather.5.cloned.1.call-update
  7.9 0.0 all-gather.7.cloned.1.call-start
  8.0 1.5 copy.27
  9.4 0.0 all-gather.7.cloned.1.call-update
  9.5 0.0 all-gather.9.cloned.1.call-start
  9.5 0.7 all-gather.9.cloned.1.call-update
  10.2 0.8 select_reduce_fusion.1
  11.0 0.0 copy-done
  11.0 0.8 gather_fusion
  11.9 1.2 select_bitcast_fusion
  13.1 16.5 %all-to-all-start = ((bf16[2,2,64,16,128]{4,3,1,0,2:T(8,128)(2,1)}), bf16[2,2,64,16,128]{4,3,1,0,2:T(8,128)(2,1)S(1)}, u32[]{:S(2)}, u32[]{:S(2)}) async-start(bf16[2,2,64,16,128]{4,3,1,0,2:T(8,128)(2,1)} %select_bitcast_fusion), calls=%async_computation | async-start | bytes 2097152 | tf_op jit(solution)/shard_map/all_to_all | solution.py:89
  29.5 0.0 all-reduce.2.cloned.1.call-start
  29.6 1.1 copy.25
  30.7 98.7 %all-gather = s32[64,1,128]{2,1,0:T(1,128)S(1)} all-gather(s32[1,1,128]{2,1,0:T(1,128)} %bitcast.79), channel_id=1, replica_groups=mesh['seq'=64,'head'=8] {'seq'}, dimensions={0}, use_global_device_ids=true | all-gather | bytes 33280 | tf_op jit(solution)/shard_map/all_gather | solution.py:30
  129.4 4.4 %fusion.7 = pred[128,8192]{0,1:T(8,128)(4,1)S(1)} fusion(s32[128]{0:T(128)S(1)} %iota_add_fusion, s32[128]{0:T(128)} %param.12, s32[8192]{0:T(1024)S(1)} %bitcast.78), kind=kLoop, calls=%fused_computation.11 | loop fusion | flops 3145728 | bytes 1082368 | tf_op jit(solution)/shard_map/and | solution.py:34
  133.8 0.0 all-gather.5.cloned.1.call-done
  133.8 4.7 %fusion = (f32[5,128]{1,0:T(8,128)S(1)}, f32[8192,128,5]{1,0,2:T(8,128)S(1)}) fusion(pred[128,8192]{0,1:T(8,128)(4,1)S(1)} %fusion.7, bf16[128,5,128]{0,2,1:T(8,128)(2,1)S(1)} %bitcast.76, bf16[8192,128]{1,0:T(8,128)(2,1)} %all-gather.5.cloned.1.call-done), kind=kOutput, calls=%fused_computation.3 | convolution fusion | flops 1357905280 | bytes 24283648 | tf_op jit(solution)/shard_map/tkgd,pkd->kgtp/dot_general | solution.py:42
  138.6 0.0 copy-start.1
  138.6 6.9 %copy-done.1 = f32[8192,128,5]{1,0,2:T(8,128)} copy-done((f32[8192,128,5]{1,0,2:T(8,128)}, f32[8192,128,5]{1,0,2:T(8,128)S(1)}, u32[]{:S(2)}) %copy-start.1) | copy-done | bytes 20971544
  145.5 5.2 %fusion.1 = f32[5,128]{1,0:T(8,128)S(1)} fusion(f32[8192,128,5]{1,0,2:T(8,128)S(1)} %get-tuple-element.7, f32[5,128]{1,0:T(8,128)S(1)} %broadcast_maximum_fusion, pred[128,8192]{0,1:T(8,128)(4,1)S(1)} %fusion.7), kind=kLoop, calls=%fused_computation.4 | loop fusion | flops 26213760 | bytes 22025216 | tf_op jit(solution)/shard_map/reduce_sum | solution.py:48
  150.7 40.7 %all-gather.7.cloned.1.call-done = bf16[8192,128]{0,1:T(8,128)(2,1)} async-done(((bf16[128,128]{0,1:T(8,128)(2,1)}), bf16[8192,128]{0,1:T(8,128)(2,1)}) %all-gather.7.cloned.1.call-update) | async-done | bytes 2097168 | tf_op jit(solution)/shard_map/all_gather | solution.py:29
  191.4 12.9 %fusion.16 = bf16[5,128,128]{1,2,0:T(8,128)(2,1)S(1)} fusion(f32[8192,128,5]{1,0,2:T(8,128)} %copy-done.1, f32[5,128]{1,0:T(8,128)S(1)} %broadcast_maximum_fusion, pred[128,8192]{0,1:T(8,128)(4,1)S(1)} %fusion.7, bf16[8192,128]{0,1:T(8,128)(2,1)} %all-gather.7.cloned.1.call-done, f32[5,128]{1,0:T(8,128)S(1)} %fusion.1), kind=kOutput, calls=%fused_computation.18 | convolution fusion | flops 1368555520 | bytes 24286208 | tf_op jit(solution)/shard_map/kgtp,pkd->kgtd/dot_general | solution.py:49
  204.3 0.0 copy-start.2
  204.4 81.0 %all-gather.9.cloned.1.call-done = bf16[640,5120]{0,1:T(8,128)(2,1)} async-done(((bf16[640,80]{0,1:T(8,128)(2,1)}), bf16[640,5120]{0,1:T(8,128)(2,1)}) %all-gather.9.cloned.1.call-update) | async-done | bytes 6553616 | tf_op jit(solution)/shard_map/all_gather | solution.py:62
  285.3 6.2 %convolution_convert_fusion = bf16[128,5120]{1,0:T(8,128)(2,1)} fusion(bf16[128,640]{0,1:T(8,128)(2,1)S(1)} %bitcast.77, bf16[640,5120]{0,1:T(8,128)(2,1)} %all-gather.9.cloned.1.call-done), kind=kOutput, calls=%fused_computation.9 | convolution fusion | flops 839516160 | bytes 8028160 | tf_op jit(solution)/shard_map/dot_general | solution.py:60
  291.5 0.0 all-reduce.2.cloned.1.call-update
  291.5 0.6 dynamic_slice.14
  292.1 0.6 dynamic_slice.15
  294.1 0.7 iota_compare_fusion.3
  294.7 0.0 all-to-all-done
  294.7 1.5 bitcast_select_fusion.1
  296.2 86.8 %all-reduce.2.cloned.1.call-done = bf16[128,5120]{1,0:T(8,128)(2,1)} async-done(((bf16[128,5120]{1,0:T(8,128)(2,1)}), bf16[128,5120]{1,0:T(8,128)(2,1)}) %all-reduce.2.cloned.1.call-update) | async-done | bytes 1310736 | tf_op jit(solution)/shard_map/psum | solution.py:66
  383.0 0.0 copy-done.2
  383.0 1.6 add_convert_fusion
  (5 shorter events, 0.1 us)
Async XLA Ops:
  7.2 3.9 copy-start
  7.2 126.6 %all-gather.5.cloned.1.call-start = ((), (), s32[]{:S(2)}) async-start(), calls=%async_computation.1 | async-start | bytes 2129920 | tf_op jit(solution)/shard_map/all_gather | solution.py:28
  7.9 183.5 %all-gather.7.cloned.1.call-start = ((), (), s32[]{:S(2)}) async-start(), calls=%async_computation.2 | async-start | bytes 2129920 | tf_op jit(solution)/shard_map/all_gather | solution.py:29
  9.5 275.9 %all-gather.9.cloned.1.call-start = ((), (), s32[]{:S(2)}) async-start(), calls=%async_computation.3 | async-start | bytes 6656000 | tf_op jit(solution)/shard_map/all_gather | solution.py:62
  13.1 281.6 %all-to-all-start = ((bf16[2,2,64,16,128]{4,3,1,0,2:T(8,128)(2,1)}), bf16[2,2,64,16,128]{4,3,1,0,2:T(8,128)(2,1)S(1)}, u32[]{:S(2)}, u32[]{:S(2)}) async-start(bf16[2,2,64,16,128]{4,3,1,0,2:T(8,128)(2,1)} %select_bitcast_fusion), calls=%async_computation | async-start | bytes 2097152 | tf_op jit(solution)/shard_map/all_to_all | solution.py:89
  29.5 353.5 %all-reduce.2.cloned.1.call-start = ((), (), s32[]{:S(2)}) async-start(), calls=%async_computation.4 | async-start | bytes 2621440 | tf_op jit(solution)/shard_map/psum | solution.py:66
  138.6 7.0 %copy-start.1 = (f32[8192,128,5]{1,0,2:T(8,128)}, f32[8192,128,5]{1,0,2:T(8,128)S(1)}, u32[]{:S(2)}) copy-start(f32[8192,128,5]{1,0,2:T(8,128)S(1)} %get-tuple-element.7) | copy-start | bytes 62914564
  204.3 178.7 %copy-start.2 = (bf16[128,640]{1,0:T(8,128)(2,1)S(1)}, bf16[128,640]{1,0:T(8,128)(2,1)}, u32[]{:S(2)}) copy-start(bf16[128,640]{1,0:T(8,128)(2,1)} %param.13) | copy-start | bytes 491524
Sparse Core Ops, SparseCore 0:
  11.3 100.3 all-gather.4
  115.5 75.8 all-gather.6
  194.7 90.5 all-gather.8
  291.6 91.3 all-reduce.1
where the time goes:
time: 392 us; the launch traced here: 391 us
  waiting for transfers between devices  210 us (54%)
  blocking collectives  98.7 us (25%)
  matrix products  23.8 us (6%)
  starting transfers between devices  16.6 us (4%)
  other arithmetic  15.4 us (4%)
  between operations  15.2 us (4%)
  local copies, waits for them, and re-layouts  11.5 us (3%)
    all_gather x1, blocking collectives, on_device(): segment_part = lax.all_gather(stretch_segments, 'seq', axis=0, tiled=True)  98.7 us
    psum x1, waiting for transfers between devices, on_device(): lax.psum(partial_value.astype(jnp.bfloat16), 'head').astype(jnp.float32)  86.8 us
    all_gather x1, waiting for transfers between devices, on_device(): lax.all_gather(out_weight, 'seq', axis=1, tiled=True)  81 us
    all_gather x1, waiting for transfers between devices, on_device(): value_part = lax.all_gather(block_value_rows, 'seq', axis=0, tiled=True)  40.7 us
    all_to_all x1, starting transfers between devices, on_device(): lax.all_to_all(outgoing, 'seq', split_axis=2, concat_axis=2, tiled=True)  16.5 us
    dot_general x1, matrix products, on_device(): jnp.einsum('kgtp,pkd->kgtd', weights.astype(jnp.bfloat16), value_three, p...  12.9 us
    unnamed x8, local copies, waits for them, and re-layouts  9.51 us
  transfers between devices with their start and end apart: 5, of which 3 were waited for; matrix products, arithmetic and copies ran while one was open for 11% of the time, Pallas kernels for 0%

commit v1 on v0

--- a/solution.py
+++ b/solution.py
@@ -26,7 +26,10 @@
     query_place = seq_place * rows + jnp.arange(rows, dtype=jnp.int32)
     scale = HEAD_SIZE ** (-0.5)
     key_part = lax.all_gather(block_key_rows, "seq", axis=0, tiled=True)
-    value_part = lax.all_gather(block_value_rows, "seq", axis=0, tiled=True)
+    n_dev = lax.axis_size("seq")
+    blocks = jnp.stack([block_value_rows for _ in range(n_dev)])
+    blocks = lax.all_to_all(blocks, "seq", split_axis=0, concat_axis=0)
+    value_part = jnp.concatenate(blocks, axis=0)
     segment_part = lax.all_gather(stretch_segments, "seq", axis=0, tiled=True)
     count = key_part.shape[0]
     key_place = jnp.arange(count, dtype=jnp.int32)

time: 392 us -> 360 us (0.918)
  waiting for transfers between devices: 210 us -> 129 us
  blocking collectives: 98.7 us -> 125 us
  starting transfers between devices: 16.6 us -> 32.1 us
  local copies, waits for them, and re-layouts: 11.5 us -> 19.1 us
    all_gather x1 -> x0, waiting for transfers between devices: 40.7 us -> none  [on_device(): value_part = lax.all_gather(block_value_rows, 'seq', axis=0, tiled=True)]
    all_gather x1, waiting for transfers between devices: 81 us -> 42.3 us  [on_device(): lax.all_gather(out_weight, 'seq', axis=1, tiled=True)]
    all_gather x1, blocking collectives: 98.7 us -> 125 us  [on_device(): segment_part = lax.all_gather(stretch_segments, 'seq', axis=0, tiled=True)]
    all_to_all x0 -> x1, starting transfers between devices: none -> 16.5 us  [on_device(): blocks = lax.all_to_all(blocks, 'seq', split_axis=0, concat_axis=0)]
    another operation x0 -> x2, local copies, waits for them, and re-layouts: none -> 4.65 us
    unnamed x8 -> x12, local copies, waits for them, and re-layouts: 9.51 us -> 8.91 us
  transfers between devices with their start and end apart: 5 -> 5, of which waited for: 3 -> 2; matrix products, arithmetic and copies ran while one was open for 11% -> 14% of each run, Pallas kernels for 0% -> 0%
where the time goes in v1:
time: 360 us; the launch traced here: 359 us
  waiting for transfers between devices  129 us (36%)
  blocking collectives  125 us (35%)
  starting transfers between devices  32.1 us (9%)
  matrix products  20.9 us (6%)
  local copies, waits for them, and re-layouts  19.1 us (5%)
  other arithmetic  17.8 us (5%)
  between operations  15.2 us (4%)
    all_gather x1, blocking collectives, on_device(): segment_part = lax.all_gather(stretch_segments, 'seq', axis=0, tiled=True)  125 us
    psum x1, waiting for transfers between devices, on_device(): lax.psum(partial_value.astype(jnp.bfloat16), 'head').astype(jnp.float32)  85.6 us
    all_gather x1, waiting for transfers between devices, on_device(): lax.all_gather(out_weight, 'seq', axis=1, tiled=True)  42.3 us
    all_to_all x1, starting transfers between devices, on_device(): blocks = lax.all_to_all(blocks, 'seq', split_axis=0, concat_axis=0)  16.5 us
    all_to_all x1, starting transfers between devices, on_device(): lax.all_to_all(outgoing, 'seq', split_axis=2, concat_axis=2, tiled=True)  15.3 us
    dot_general x1, matrix products, on_device(): jnp.einsum('kgtp,pkd->kgtd', weights.astype(jnp.bfloat16), value_three, p...  9.71 us
    unnamed x12, local copies, waits for them, and re-layouts  8.91 us
  transfers between devices with their start and end apart: 5, of which 2 were waited for; matrix products, arithmetic and copies ran while one was open for 14% of the time, Pallas kernels for 0%

profile of v1, /device:TPU:16, one launch (start us, length us, event | category | flops | bytes accessed | tf_op | source)
XLA Modules:
  0.0 359.0 jit_solution(18368750281423588873)
XLA Ops:
  7.2 0.0 copy-start
  7.2 0.0 copy-start.4
  7.2 0.0 all-gather.4.cloned.1.call-start
  7.2 0.7 all-gather.4.cloned.1.call-update
  7.9 0.0 all-gather.6.cloned.1.call-start
  8.0 0.7 all-gather.6.cloned.1.call-update
  8.7 0.9 copy.28
  9.5 1.8 stack.2
  11.4 16.5 %all-to-all-start = ((bf16[64,128,128]{1,2,0:T(8,128)(2,1)}), bf16[64,128,128]{1,2,0:T(8,128)(2,1)S(1)}, u32[]{:S(2)}, u32[]{:S(2)}) async-start(bf16[64,128,128]{1,2,0:T(8,128)(2,1)} %stack.2), calls=%async_computation | async-start | bytes 4194304 | tf_op jit(solution)/shard_map/all_to_all | solution.py:31
  27.9 1.1 copy.26
  28.9 0.8 select_reduce_fusion.1
  29.8 0.0 copy-done
  29.8 1.7 gather_fusion
  31.5 124.5 %all-gather = s32[64,1,128]{2,1,0:T(1,128)S(1)} all-gather(s32[1,1,128]{2,1,0:T(1,128)} %bitcast.74), channel_id=1, replica_groups=mesh['seq'=64,'head'=8] {'seq'}, dimensions={0}, use_global_device_ids=true | all-gather | bytes 33280 | tf_op jit(solution)/shard_map/all_gather | solution.py:33
  156.0 2.4 select_bitcast_fusion
  158.5 0.0 copy-done.4
  158.5 4.4 %fusion.7 = pred[128,8192]{0,1:T(8,128)(4,1)} fusion(s32[128]{0:T(128)S(1)} %iota_add_fusion, s32[128]{0:T(128)S(1)} %copy-done.4, s32[8192]{0:T(1024)S(1)} %bitcast.73), kind=kLoop, calls=%fused_computation.11 | loop fusion | flops 3145728 | bytes 1082368 | tf_op jit(solution)/shard_map/and | solution.py:37
  162.9 0.0 all-to-all-done
  162.9 15.3 %all-to-all-start.1 = ((bf16[2,2,64,16,128]{4,3,1,0,2:T(8,128)(2,1)}), bf16[2,2,64,16,128]{4,3,1,0,2:T(8,128)(2,1)}, u32[]{:S(2)}, u32[]{:S(2)}) async-start(bf16[2,2,64,16,128]{4,3,1,0,2:T(8,128)(2,1)} %select_bitcast_fusion), calls=%async_computation.1 | async-start | bytes 2097152 | tf_op jit(solution)/shard_map/all_to_all | solution.py:92
  178.2 0.2 all-reduce.2.cloned.1.call-start
  178.4 2.7 copy.29
  181.1 2.8 reshape.213
  183.9 0.0 all-gather.4.cloned.1.call-done
  183.9 0.0 copy-start.2
  184.0 5.0 %fusion = (f32[5,128]{1,0:T(8,128)S(1)}, f32[8192,128,5]{1,0,2:T(8,128)S(1)}) fusion(pred[128,8192]{0,1:T(8,128)(4,1)} %fusion.7, bf16[128,5,128]{0,2,1:T(8,128)(2,1)S(1)} %bitcast.71, bf16[8192,128]{1,0:T(8,128)(2,1)} %all-gather.4.cloned.1.call-done), kind=kOutput, calls=%fused_computation.3 | convolution fusion | flops 1357905280 | bytes 24283648 | tf_op jit(solution)/shard_map/tkgd,pkd->kgtp/dot_general | solution.py:45
  189.0 0.0 copy-start.1
  189.0 6.9 %copy-done.1 = f32[8192,128,5]{1,0,2:T(8,128)} copy-done((f32[8192,128,5]{1,0,2:T(8,128)}, f32[8192,128,5]{1,0,2:T(8,128)S(1)}, u32[]{:S(2)}) %copy-start.1) | copy-done | bytes 20971544
  195.9 0.0 copy-done.2
  195.9 5.2 %fusion.1 = f32[5,128]{1,0:T(8,128)S(1)} fusion(f32[8192,128,5]{1,0,2:T(8,128)S(1)} %get-tuple-element.7, f32[5,128]{1,0:T(8,128)S(1)} %broadcast_maximum_fusion, pred[128,8192]{0,1:T(8,128)(4,1)S(1)} %copy-done.2), kind=kLoop, calls=%fused_computation.4 | loop fusion | flops 26213760 | bytes 22025216 | tf_op jit(solution)/shard_map/reduce_sum | solution.py:51
  201.1 9.7 %fusion.13 = bf16[5,128,128]{1,2,0:T(8,128)(2,1)S(1)} fusion(bf16[8192,128,1]{0,1,2:T(8,128)(2,1)S(1)} %reshape.213, f32[8192,128,5]{1,0,2:T(8,128)} %copy-done.1, f32[5,128]{1,0:T(8,128)S(1)} %broadcast_maximum_fusion, pred[128,8192]{0,1:T(8,128)(4,1)S(1)} %copy-done.2, f32[5,128]{1,0:T(8,128)S(1)} %fusion.1), kind=kOutput, calls=%fused_computation.17 | convolution fusion | flops 1368555520 | bytes 24286208 | tf_op jit(solution)/shard_map/kgtp,pkd->kgtd/dot_general | solution.py:52
  210.8 0.0 copy-start.3
  210.9 42.3 %all-gather.6.cloned.1.call-done = bf16[640,5120]{0,1:T(8,128)(2,1)} async-done(((bf16[640,80]{0,1:T(8,128)(2,1)}), bf16[640,5120]{0,1:T(8,128)(2,1)}) %all-gather.6.cloned.1.call-update) | async-done | bytes 6553616 | tf_op jit(solution)/shard_map/all_gather | solution.py:65
  253.1 6.2 %convolution_convert_fusion = bf16[128,5120]{1,0:T(8,128)(2,1)} fusion(bf16[128,640]{0,1:T(8,128)(2,1)S(1)} %bitcast.72, bf16[640,5120]{0,1:T(8,128)(2,1)} %all-gather.6.cloned.1.call-done), kind=kOutput, calls=%fused_computation.9 | convolution fusion | flops 839516160 | bytes 8028160 | tf_op jit(solution)/shard_map/dot_general | solution.py:63
  259.3 0.0 all-reduce.2.cloned.1.call-update
  259.3 0.6 dynamic_slice.14
  259.9 0.6 dynamic_slice.15
  261.8 0.7 iota_compare_fusion.3
  262.5 0.0 all-to-all-done.1
  262.5 2.7 bitcast_select_fusion.1
  265.2 85.6 %all-reduce.2.cloned.1.call-done = bf16[128,5120]{1,0:T(8,128)(2,1)} async-done(((bf16[128,5120]{1,0:T(8,128)(2,1)}), bf16[128,5120]{1,0:T(8,128)(2,1)}) %all-reduce.2.cloned.1.call-update) | async-done | bytes 1310736 | tf_op jit(solution)/shard_map/psum | solution.py:69
  350.8 0.0 copy-done.3
  350.8 1.6 add_convert_fusion
  (5 shorter events, 0.1 us)
Async XLA Ops:
  7.2 22.6 %copy-start = (bf16[2,2,32,16,128]{4,3,2,1,0:T(8,128)(2,1)S(1)}, bf16[2,2,32,16,128]{4,3,2,1,0:T(8,128)(2,1)}, u32[]{:S(2)}) copy-start(bf16[2,2,32,16,128]{4,3,2,1,0:T(8,128)(2,1)} %param.15) | copy-start | bytes 1572868
  7.2 151.3 %copy-start.4 = (s32[128]{0:T(128)S(1)}, s32[128]{0:T(128)}, u32[]{:S(2)}) copy-start(s32[128]{0:T(128)} %param.12) | copy-start | bytes 1540
  7.2 176.7 %all-gather.4.cloned.1.call-start = ((), (), s32[]{:S(2)}) async-start(), calls=%async_computation.2 | async-start | bytes 2129920 | tf_op jit(solution)/shard_map/all_gather | solution.py:28
  7.9 245.2 %all-gather.6.cloned.1.call-start = ((), (), s32[]{:S(2)}) async-start(), calls=%async_computation.3 | async-start | bytes 6656000 | tf_op jit(solution)/shard_map/all_gather | solution.py:65
  11.4 151.5 %all-to-all-start = ((bf16[64,128,128]{1,2,0:T(8,128)(2,1)}), bf16[64,128,128]{1,2,0:T(8,128)(2,1)S(1)}, u32[]{:S(2)}, u32[]{:S(2)}) async-start(bf16[64,128,128]{1,2,0:T(8,128)(2,1)} %stack.2), calls=%async_computation | async-start | bytes 4194304 | tf_op jit(solution)/shard_map/all_to_all | solution.py:31
  162.9 99.6 %all-to-all-start.1 = ((bf16[2,2,64,16,128]{4,3,1,0,2:T(8,128)(2,1)}), bf16[2,2,64,16,128]{4,3,1,0,2:T(8,128)(2,1)}, u32[]{:S(2)}, u32[]{:S(2)}) async-start(bf16[2,2,64,16,128]{4,3,1,0,2:T(8,128)(2,1)} %select_bitcast_fusion), calls=%async_computation.1 | async-start | bytes 2097152 | tf_op jit(solution)/shard_map/all_to_all | solution.py:92
  178.2 172.6 %all-reduce.2.cloned.1.call-start = ((), (), s32[]{:S(2)}) async-start(), calls=%async_computation.4 | async-start | bytes 2621440 | tf_op jit(solution)/shard_map/psum | solution.py:69
  183.9 12.0 %copy-start.2 = (pred[128,8192]{0,1:T(8,128)(4,1)S(1)}, pred[128,8192]{0,1:T(8,128)(4,1)}, u32[]{:S(2)}) copy-start(pred[128,8192]{0,1:T(8,128)(4,1)} %fusion.7) | copy-start | bytes 3145732
  189.0 7.0 %copy-start.1 = (f32[8192,128,5]{1,0,2:T(8,128)}, f32[8192,128,5]{1,0,2:T(8,128)S(1)}, u32[]{:S(2)}) copy-start(f32[8192,128,5]{1,0,2:T(8,128)S(1)} %get-tuple-element.7) | copy-start | bytes 62914564
  210.8 140.0 %copy-start.3 = (bf16[128,640]{1,0:T(8,128)(2,1)S(1)}, bf16[128,640]{1,0:T(8,128)(2,1)}, u32[]{:S(2)}) copy-start(bf16[128,640]{1,0:T(8,128)(2,1)} %param.13) | copy-start | bytes 491524
Sparse Core Ops, SparseCore 0:
  11.3 122.2 all-gather.3
  136.9 116.1 all-gather.5
  259.4 91.3 all-reduce.1
